TPU v7x, 32 devices: a whole 2x2x4 slice. The times are simulated.
32 devices in a mesh: row: 4 (over y, core), col: 8 (over z, x).
Axes of the slice: x: 2, y: 2, z: 4, core: 2. Of those that a mesh axis runs over, the one named last changes fastest.
Arguments:
- ancestor_inverse: float32 [12288, 12288], P('row', 'col')
- factor: bfloat16 [3, 12288, 512], P(None, ('row', 'col')), may hold values from -0.5 to 0.5
- coupling: float32 [3, 512, 512], replicated, may hold values from -0.25 to 0.25
- diagonal_inverse: float32 [3, 512, 512], replicated, may hold values from -6 to 6
- ancestors: int32 [3, 24], replicated, may hold values from -1 to 23, as said below
Outputs:
- block_columns: float32 [3, 12288, 512], P(None, ('row', 'col'))
- block_rows: float32 [3, 12288, 512], P(None, ('col', 'row'))
- node_blocks: float32 [3, 3, 512, 512], replicated
Inputs may be any that keep to these rules, and one draw needn't show every extreme that they name: `ancestors`: row k lists the ancestor block rows of supernode k, blocks of 512 rows: distinct indices in increasing order, then -1 in the slots left. Every block is listed by some supernode.
All inputs are finite; a program needn't handle non-finite values.
Results may differ from a plain program's by a relative error of at most 0.0003.
Values may be sent and summed in bfloat16 or wider, within the bound.
No kernel may reach another device: no remote copies, remote signals or barrier semaphores. Data moves between devices by JAX's collectives and lax.ppermute only.
A program may use at most 128 MiB of HBM per device.

v0:
```python
import jax
import jax.numpy as jnp
from jax import lax
from jax.sharding import PartitionSpec as P

highest = lax.Precision.HIGHEST


def broadcast(value, axis, source):
    kept = jnp.where(lax.axis_index(axis) == source, value, 0).astype(value.dtype)
    return lax.psum(kept, axis)


def matmul(left, right):
    return jnp.dot(left, right, precision=highest)


def left_dot(left, right):
    return lax.dot_general(left, right, (((0,), (0,)), ((), ())), precision=highest)


def pair_index(later, earlier):
    return later * (later - 1) // 2 + earlier


def local(ancestor_inverse, factor, coupling, diagonal_inverse, ancestors):
    col_count = lax.axis_size("col")
    row_index = lax.axis_index("row")
    col_index = lax.axis_index("col")
    nodes_total, piece_rows, sn_width = factor.shape
    rows_here, cols_here = ancestor_inverse.shape
    group_ratio = rows_here // cols_here
    first_row = (row_index * col_count + col_index) * piece_rows
    block_of_row = (first_row + jnp.arange(piece_rows, dtype=jnp.int32)) // sn_width
    source_row = col_index // group_ratio
    block_start = col_index % group_ratio * cols_here
    row_layout = []
    col_layout = []
    solved = {}
    for current in range(nodes_total):
        listed = jnp.any(ancestors[current][:, None] == block_of_row[None, :], axis=0)
        lower_part = jnp.where(listed[:, None], factor[current], jnp.zeros_like(factor[current]))
        lower_rows = lax.all_gather(lower_part, "col", axis=0, tiled=True)
        own_block = lax.dynamic_slice_in_dim(lower_rows, block_start, cols_here, 0)
        lower_cols = broadcast(own_block, "row", source_row).astype(jnp.float32)
        lower_here = lower_part.astype(jnp.float32)
        product_sum = lax.psum_scatter(
            matmul(ancestor_inverse, lower_cols), "col", scatter_dimension=0, tiled=True
        )
        for earlier in range(current):
            product_sum = product_sum + matmul(
                row_layout[earlier], coupling[pair_index(current, earlier)]
            )
        column = -product_sum
        stacked = jnp.concatenate(row_layout + [column], axis=1)
        summed = lax.psum(left_dot(lower_here, stacked), ("row", "col"))
        crosses = [
            summed[:, earlier * sn_width : (earlier + 1) * sn_width] for earlier in range(current)
        ]
        self_term = summed[:, current * sn_width : (current + 1) * sn_width]
        for earlier in range(current):
            block_value = -crosses[earlier].T
            for inner in range(current):
                block_value = block_value - matmul(
                    solved[earlier, inner], coupling[pair_index(current, inner)]
                )
            solved[earlier, current] = block_value
            solved[current, earlier] = block_value.T
        diag_value = diagonal_inverse[current] - self_term
        for earlier in range(current):
            diag_value = diag_value - left_dot(
                coupling[pair_index(current, earlier)], solved[earlier, current]
            )
        solved[current, current] = diag_value
        rows_float = lower_rows.astype(jnp.float32)
        mirror = lax.psum_scatter(
            left_dot(ancestor_inverse, rows_float), "row", scatter_dimension=0, tiled=True
        )
        for earlier in range(current):
            mirror = mirror + matmul(col_layout[earlier], coupling[pair_index(current, earlier)])
        col_layout.append(-mirror)
        row_layout.append(column)
    finished = jnp.stack(row_layout)
    mirrored_all = jnp.stack(col_layout)
    node_blocks = jnp.stack(
        [
            jnp.stack([solved[first_node, second_node] for second_node in range(nodes_total)])
            for first_node in range(nodes_total)
        ]
    )
    return (finished, mirrored_all, node_blocks)


def solution(mesh):
    placed = (P("row", "col"), P(None, ("row", "col"), None), P(), P(), P())
    return jax.shard_map(
        local,
        mesh=mesh,
        in_specs=placed,
        out_specs=(P(None, ("row", "col"), None), P(None, ("col", "row"), None), P()),
        check_vma=False,
    )
```

profile of v0, /device:TPU:0, one launch (start us, length us, event | category | flops | bytes accessed | tf_op | source)
XLA Modules:
  0.0 1007.5 jit_solution(5974017174490358877)
XLA Ops:
  7.2 0.8 slice_bitcast_fusion.2
  8.1 2.5 bitcast_select_fusion.1
  10.7 0.7 all-gather.4.cloned.1.call-update
  11.5 0.7 all-gather.6.cloned.1.call-update
  12.2 61.3 %all-gather.8.cloned.1.call-done = bf16[3072,512]{1,0:T(8,128)(2,1)} async-done(((bf16[384,512]{1,0:T(8,128)(2,1)}), bf16[3072,512]{1,0:T(8,128)(2,1)}) %all-gather.8.cloned.1.call-update) | async-done | bytes 3145744 | tf_op jit(solution)/shard_map/all_gather | solution.py:43
  73.6 2.8 dynamic-slice_select_fusion
  76.4 58.1 %all-gather.4.cloned.1.call-done = bf16[3072,512]{1,0:T(8,128)(2,1)} async-done(((bf16[384,512]{1,0:T(8,128)(2,1)}), bf16[3072,512]{1,0:T(8,128)(2,1)}) %all-gather.4.cloned.1.call-update) | async-done | bytes 3145744 | tf_op jit(solution)/shard_map/all_gather | solution.py:43
  134.5 2.8 dynamic-slice_select_fusion.2
  137.3 58.1 %all-gather.6.cloned.1.call-done = bf16[3072,512]{1,0:T(8,128)(2,1)} async-done(((bf16[384,512]{1,0:T(8,128)(2,1)}), bf16[3072,512]{1,0:T(8,128)(2,1)}) %all-gather.6.cloned.1.call-update) | async-done | bytes 3145744 | tf_op jit(solution)/shard_map/all_gather | solution.py:43
  195.4 2.8 dynamic-slice_select_fusion.1
  198.3 92.8 %all-reduce.7.cloned.1.call-done = (bf16[1536,512]{1,0:T(8,128)(2,1)}, bf16[1536,512]{1,0:T(8,128)(2,1)}, bf16[1536,512]{1,0:T(8,128)(2,1)}) async-done(((bf16[1536,512]{1,0:T(8,128)(2,1)}, bf16[1536,512]{1,0:T(8,128)(2,1)}, bf16[1536,512]{1,0:T(8,128)(2,1)}), (bf16[1536,512]{1,0:T(8,128)(2,1)}, bf16[1536,512]{1,0:T(8,128)(2,1)}, bf16[1536,512]{1,0:T(8,128)(2,1)})) %all-reduce.7.cloned.1.call-update) | async-done | bytes 4718608 | tf_op jit(solution)/shard_map/psum | solution.py:11
  291.1 22.4 %convolution_bitcast_fusion.2 = f32[3072,512]{0,1:T(8,128)} fusion(bf16[1536,512]{1,0:T(8,128)(2,1)} %get-tuple-element.16, f32[3072,1536]{1,0:T(8,128)} %param.5), kind=kOutput, calls=%fused_computation.3 | convolution fusion | flops 28991029248 | bytes 26738688 | tf_op jit(solution)/shard_map/dot_general | solution.py:15
  313.5 1.3 copy-done.30
  314.9 21.8 %convolution_bitcast_fusion.1 = f32[3072,512]{0,1:T(8,128)} fusion(bf16[1536,512]{1,0:T(8,128)(2,1)S(1)} %copy-done.30, f32[3072,1536]{1,0:T(8,128)} %param.5), kind=kOutput, calls=%fused_computation.2 | convolution fusion | flops 28991029248 | bytes 26738688 | tf_op jit(solution)/shard_map/dot_general | solution.py:15
  336.7 0.5 reduce-scatter.11.cloned.1.call-start
  337.2 0.9 copy-done.29
  338.1 21.8 %convolution_bitcast_fusion = f32[3072,512]{0,1:T(8,128)} fusion(bf16[1536,512]{1,0:T(8,128)(2,1)S(1)} %copy-done.29, f32[3072,1536]{1,0:T(8,128)} %param.5), kind=kOutput, calls=%fused_computation.1 | convolution fusion | flops 28991029248 | bytes 26738688 | tf_op jit(solution)/shard_map/dot_general | solution.py:15
  360.0 1.9 copy-done.28
  361.8 19.7 %convolution_bitcast_fusion.3 = f32[1536,512]{0,1:T(8,128)} fusion(bf16[3072,512]{1,0:T(8,128)(2,1)S(1)} %copy-done.28, f32[3072,1536]{1,0:T(8,128)} %param.5), kind=kOutput, calls=%fused_computation.4 | convolution fusion | flops 28991029248 | bytes 25165824 | tf_op jit(solution)/shard_map/dot_general | solution.py:19
  381.8 1.7 copy-done.27
  383.5 19.9 %convolution_bitcast_fusion.5 = f32[1536,512]{0,1:T(8,128)} fusion(bf16[3072,512]{1,0:T(8,128)(2,1)S(1)} %copy-done.27, f32[3072,1536]{1,0:T(8,128)} %param.5), kind=kOutput, calls=%fused_computation.6 | convolution fusion | flops 28991029248 | bytes 25165824 | tf_op jit(solution)/shard_map/dot_general | solution.py:19
  403.5 1.8 copy-done.26
  405.3 19.7 %convolution_bitcast_fusion.4 = f32[1536,512]{0,1:T(8,128)} fusion(bf16[3072,512]{1,0:T(8,128)(2,1)S(1)} %copy-done.26, f32[3072,1536]{1,0:T(8,128)} %param.5), kind=kOutput, calls=%fused_computation.5 | convolution fusion | flops 28991029248 | bytes 25165824 | tf_op jit(solution)/shard_map/dot_general | solution.py:19
  425.3 6.5 reduce-scatter.7.cloned.1.call-done
  431.8 2.4 fusion.73
  434.2 3.3 fusion.64
  437.5 115.1 %reduce-scatter.9.cloned.1.call-done = f32[384,512]{0,1:T(8,128)} async-done(((f32[3072,512]{0,1:T(8,128)}), f32[384,512]{0,1:T(8,128)}) %reduce-scatter.9.cloned.1.call-update) | async-done | bytes 786448 | tf_op jit(solution)/shard_map/reduce_scatter | solution.py:47
  552.6 3.4 fusion.14
  555.9 0.9 copy-done.3
  556.9 3.1 fusion.6
  560.0 114.0 %reduce-scatter.11.cloned.1.call-done = f32[384,512]{0,1:T(8,128)} async-done(((f32[3072,512]{0,1:T(8,128)}), f32[384,512]{0,1:T(8,128)}) %reduce-scatter.11.cloned.1.call-update) | async-done | bytes 786448 | tf_op jit(solution)/shard_map/reduce_scatter | solution.py:47
  674.0 3.3 convolution_add_fusion.4
  677.4 1.9 fusion.15
  679.3 0.9 copy-done.12
  680.2 4.5 fusion
  684.7 2.3 slice.74
  687.0 2.9 copy.65
  690.0 23.6 %reduce-scatter.17.cloned.1.call-done = f32[384,512]{0,1:T(8,128)} async-done(((f32[1536,512]{0,1:T(8,128)}), f32[384,512]{0,1:T(8,128)}) %reduce-scatter.17.cloned.1.call-update) | async-done | bytes 786448 | tf_op jit(solution)/shard_map/reduce_scatter | solution.py:76
  713.6 40.3 %reduce-scatter.13.cloned.1.call-done = f32[384,512]{0,1:T(8,128)} async-done(((f32[1536,512]{0,1:T(8,128)}), f32[384,512]{0,1:T(8,128)}) %reduce-scatter.13.cloned.1.call-update) | async-done | bytes 786448 | tf_op jit(solution)/shard_map/reduce_scatter | solution.py:76
  753.9 4.1 convolution_add_fusion.1
  758.0 36.0 %reduce-scatter.15.cloned.1.call-done = f32[384,512]{0,1:T(8,128)} async-done(((f32[1536,512]{0,1:T(8,128)}), f32[384,512]{0,1:T(8,128)}) %reduce-scatter.15.cloned.1.call-update) | async-done | bytes 786448 | tf_op jit(solution)/shard_map/reduce_scatter | solution.py:76
  794.0 3.4 fusion.16
  797.4 1.9 fusion.18
  799.4 1.6 pad_maximum_fusion.2
  800.9 3.0 copy.51
  804.0 3.2 pad_maximum_fusion.1
  807.1 3.2 copy.50
  810.3 146.5 %all-reduce.5.cloned.1.call-done = (f32[512,1536]{1,0:T(8,128)}, f32[512,512]{1,0:T(8,128)}, f32[512,1024]{0,1:T(8,128)}) async-done(((f32[512,1536]{1,0:T(8,128)}, f32[512,512]{1,0:T(8,128)}, f32[512,1024]{0,1:T(8,128)}), (f32[512,1536]{1,0:T(8,128)}, f32[512,512]{1,0:T(8,128)}, f32[512,1024]{0,1:T(8,128)})) %all-reduce.5.cloned.1.call-update) | async-done | bytes 6291472 | tf_op jit(solution)/shard_map/psum | solution.py:56
  956.9 3.6 fusion.34
  960.5 3.2 bitcast_subtract_fusion.7
  963.7 1.9 fusion.32
  965.6 1.9 fusion.27
  967.5 2.0 fusion.13
  969.5 1.0 copy-done.8
  970.5 1.9 fusion.25
  972.4 3.3 fusion.12
  975.7 2.3 fusion.20
  978.0 2.3 fusion.70
  980.3 2.5 copy.39
  982.9 5.3 fusion.11
  988.2 2.0 maximum_bitcast_fusion.1
  990.1 2.4 copy.49
  992.6 2.3 maximum_bitcast_fusion.2
  995.6 5.1 pad_maximum_fusion
  (77 shorter events, 1.9 us)
Async XLA Ops:
  7.2 66.4 %all-gather.8.cloned.1.call-start = ((), (), s32[]{:S(2)}) async-start(), calls=%async_computation.10 | async-start | bytes 3538944 | tf_op jit(solution)/shard_map/all_gather | solution.py:43
  10.7 123.8 %all-gather.4.cloned.1.call-start = ((), (), s32[]{:S(2)}) async-start(), calls=%async_computation.6 | async-start | bytes 3538944 | tf_op jit(solution)/shard_map/all_gather | solution.py:43
  11.4 183.9 %all-gather.6.cloned.1.call-start = ((), (), s32[]{:S(2)}) async-start(), calls=%async_computation.8 | async-start | bytes 3538944 | tf_op jit(solution)/shard_map/all_gather | solution.py:43
  12.2 278.9 %all-reduce.7.cloned.1.call-start = ((), (), s32[]{:S(2)}) async-start(), calls=%async_computation.16 | async-start | bytes 9437184 | tf_op jit(solution)/shard_map/psum | solution.py:11
  198.2 233.6 %reduce-scatter.7.cloned.1.call-start = ((), (), s32[]{:S(2)}) async-start(), calls=%async_computation.7 | async-start | bytes 7077888 | tf_op jit(solution)/shard_map/reduce_scatter | solution.py:47
  313.5 1.4 copy-start.30
  313.5 239.1 %reduce-scatter.9.cloned.1.call-start = ((), (), s32[]{:S(2)}) async-start(), calls=%async_computation.9 | async-start | bytes 7077888 | tf_op jit(solution)/shard_map/reduce_scatter | solution.py:47
  336.7 1.4 copy-start.29
  336.7 337.3 %reduce-scatter.11.cloned.1.call-start = ((), (), s32[]{:S(2)}) async-start(), calls=%async_computation.11 | async-start | bytes 7077888 | tf_op jit(solution)/shard_map/reduce_scatter | solution.py:47
  359.9 1.9 copy-start.28
  359.9 353.6 %reduce-scatter.17.cloned.1.call-start = ((), (), s32[]{:S(2)}) async-start(), calls=%async_computation.14 | async-start | bytes 3932160 | tf_op jit(solution)/shard_map/reduce_scatter | solution.py:76
  381.6 2.0 copy-start.27
  381.6 372.2 %reduce-scatter.13.cloned.1.call-start = ((), (), s32[]{:S(2)}) async-start(), calls=%async_computation.12 | async-start | bytes 3932160 | tf_op jit(solution)/shard_map/reduce_scatter | solution.py:76
  403.4 1.9 copy-start.26
  403.5 390.5 %reduce-scatter.15.cloned.1.call-start = ((), (), s32[]{:S(2)}) async-start(), calls=%async_computation.13 | async-start | bytes 3932160 | tf_op jit(solution)/shard_map/reduce_scatter | solution.py:76
  425.0 9.2 copy-start.23
  425.0 127.6 %copy-start = (f32[3,512,512]{2,1,0:T(8,128)S(1)}, f32[3,512,512]{2,1,0:T(8,128)}, u32[]{:S(2)}) copy-start(f32[3,512,512]{2,1,0:T(8,128)} %param.7) | copy-start | bytes 9437188
  425.0 531.9 %all-reduce.5.cloned.1.call-start = ((), (), s32[]{:S(2)}) async-start(), calls=%async_computation.15 | async-start | bytes 12582912 | tf_op jit(solution)/shard_map/psum | solution.py:56
  437.5 119.4 %copy-start.24 = (bf16[384,512]{1,0:T(8,128)(2,1)S(1)}, bf16[384,512]{1,0:T(8,128)(2,1)}, u32[]{:S(2)}) copy-start(bf16[384,512]{1,0:T(8,128)(2,1)} %get-tuple-element.22) | copy-start | bytes 1179652
  552.6 4.3 copy-start.13
  555.9 0.9 copy-start.3
  560.0 120.2 %copy-start.16 = (bf16[384,512]{1,0:T(8,128)(2,1)S(1)}, bf16[384,512]{1,0:T(8,128)(2,1)}, u32[]{:S(2)}) copy-start(bf16[384,512]{1,0:T(8,128)(2,1)} %get-tuple-element.24) | copy-start | bytes 1179652
  674.0 3.4 copy-start.4
  674.0 6.2 copy-start.14
  679.2 0.9 copy-start.12
  794.0 3.4 copy-start.25
  794.0 5.3 copy-start.15
  956.9 3.6 copy-start.10
  956.9 3.6 copy-start.11
  963.7 3.8 copy-start.1
  963.7 3.8 copy-start.17
  963.7 3.8 copy-start.18
  965.6 12.4 %copy-start.5 = (f32[512,512]{0,1:T(8,128)}, f32[512,512]{0,1:T(8,128)S(1)}, u32[]{:S(2)}) copy-start(f32[512,512]{0,1:T(8,128)S(1)} %fusion.32) | copy-start | bytes 3145732
  967.5 4.9 copy-start.7
  969.5 1.0 copy-start.8
  972.4 5.6 copy-start.6
  982.9 5.3 copy-start.9
  982.9 5.3 copy-start.21
  982.9 5.3 copy-start.22
  992.5 2.4 copy-start.2
  992.5 2.5 copy-start.19
  992.5 2.8 copy-start.20
Sparse Core Ops, SparseCore 0:
  10.8 62.7 all-gather.7
  75.7 58.6 all-gather.3
  136.7 58.6 all-gather.5
  198.3 92.7 all-reduce.6
  313.6 118.1 reduce-scatter.6
  435.2 117.2 reduce-scatter.8
  556.7 117.2 reduce-scatter.10
  676.5 36.9 reduce-scatter.16
  716.1 37.7 reduce-scatter.12
  756.2 37.7 reduce-scatter.14
  800.5 156.3 all-reduce.4
where the time goes:
time: 1020 us; the launch traced here: 1010 us
  waiting for transfers between devices  754 us (74%)
  matrix products  177 us (17%)
  other arithmetic  32.6 us (3%)
  local copies, waits for them, and re-layouts  28.1 us (3%)
  between operations  14.5 us (1%)
    reduce_scatter x3, waiting for transfers between devices, local(): lax.psum_scatter(matmul(ancestor_inverse, lower_cols), 'col', scatter_dim...  236 us
    all_gather x3, waiting for transfers between devices, local(): lower_rows = lax.all_gather(lower_part, 'col', axis=0, tiled=True)  177 us
    psum x1, waiting for transfers between devices, local(): summed = lax.psum(left_dot(lower_here, stacked), ('row', 'col'))  147 us
    reduce_scatter x3, waiting for transfers between devices, local(): lax.psum_scatter(left_dot(ancestor_inverse, rows_float), 'row', scatter_d...  99.9 us
    dot_general x14, matrix products, matmul(): return jnp.dot(left, right, precision=highest)  96.3 us
    psum x1, waiting for transfers between devices, broadcast(): return lax.psum(kept, axis)  92.8 us
    dot_general x9, matrix products, left_dot(): lax.dot_general(left, right, (((0,), (0,)), ((), ())), precision=highest)  80.7 us
  transfers between devices with their start and end apart: 11, of which 11 were waited for; matrix products, arithmetic and copies ran while one was open for 15% of the time, Pallas kernels for 0%

commit v1 on v0

--- a/solution.py
+++ b/solution.py
@@ -4,6 +4,12 @@
 from jax.sharding import PartitionSpec as P
 
 highest = lax.Precision.HIGHEST
+
+
+def search_the_spot(unit):
+    o_now = lax.psum(unit, "col")
+    base_arr = lax.psum(o_now, "row")
+    return base_arr
 
 
 def broadcast(value, axis, source):
@@ -53,7 +59,7 @@
             )
         column = -product_sum
         stacked = jnp.concatenate(row_layout + [column], axis=1)
-        summed = lax.psum(left_dot(lower_here, stacked), ("row", "col"))
+        summed = search_the_spot(left_dot(lower_here, stacked))
         crosses = [
             summed[:, earlier * sn_width : (earlier + 1) * sn_width] for earlier in range(current)
         ]

time: 1020 us -> 1200 us (1.18)
  waiting for transfers between devices: 754 us -> 934 us
    psum x1 -> x2, waiting for transfers between devices: 147 us -> 251 us  [the longest x1 146 us: search_the_spot(): o_now = lax.psum(unit, 'col')]
    reduce_scatter x3, waiting for transfers between devices: 236 us -> 299 us  [local(): lax.psum_scatter(matmul(ancestor_inverse, lower_cols), 'col', scatter_dim...]
  transfers between devices with their start and end apart: 11 -> 12, of which waited for: 11 -> 12; matrix products, arithmetic and copies ran while one was open for 15% -> 12% of each run, Pallas kernels for 0% -> 0%
where the time goes in v1:
time: 1200 us; the launch traced here: 1190 us
  waiting for transfers between devices  934 us (78%)
  matrix products  180 us (15%)
  other arithmetic  31.1 us (3%)
  local copies, waits for them, and re-layouts  20.3 us (2%)
  between operations  15 us (1%)
  starting transfers between devices  12.7 us (1%)
    reduce_scatter x3, waiting for transfers between devices, local(): lax.psum_scatter(matmul(ancestor_inverse, lower_cols), 'col', scatter_dim...  299 us
    all_gather x3, waiting for transfers between devices, local(): lower_rows = lax.all_gather(lower_part, 'col', axis=0, tiled=True)  177 us
    psum x1, waiting for transfers between devices, search_the_spot(): o_now = lax.psum(unit, 'col')  146 us
    reduce_scatter x3, waiting for transfers between devices, local(): lax.psum_scatter(left_dot(ancestor_inverse, rows_float), 'row', scatter_d...  111 us
    psum x1, waiting for transfers between devices, search_the_spot(): base_arr = lax.psum(o_now, 'row')  105 us
    dot_general x14, matrix products, matmul(): return jnp.dot(left, right, precision=highest)  97.1 us
    psum x1, waiting for transfers between devices, broadcast(): return lax.psum(kept, axis)  92.8 us
    dot_general x9, matrix products, left_dot(): lax.dot_general(left, right, (((0,), (0,)), ((), ())), precision=highest)  82.8 us
  transfers between devices with their start and end apart: 12, of which 12 were waited for; matrix products, arithmetic and copies ran while one was open for 12% of the time, Pallas kernels for 0%

profile of v1, /device:TPU:0, one launch (start us, length us, event | category | flops | bytes accessed | tf_op | source)
XLA Modules:
  0.0 1192.6 jit_solution(3969772240734581204)
XLA Ops:
  7.2 0.8 slice_bitcast_fusion.2
  8.1 2.5 bitcast_select_fusion.1
  10.7 0.7 all-gather.4.cloned.1.call-update
  11.4 0.7 all-gather.6.cloned.1.call-update
  12.2 61.3 %all-gather.8.cloned.1.call-done = bf16[3072,512]{1,0:T(8,128)(2,1)} async-done(((bf16[384,512]{1,0:T(8,128)(2,1)}), bf16[3072,512]{1,0:T(8,128)(2,1)}) %all-gather.8.cloned.1.call-update) | async-done | bytes 3145744 | tf_op jit(solution)/shard_map/all_gather | solution.py:49
  73.5 2.8 dynamic-slice_select_fusion
  76.3 58.1 %all-gather.4.cloned.1.call-done = bf16[3072,512]{1,0:T(8,128)(2,1)} async-done(((bf16[384,512]{1,0:T(8,128)(2,1)}), bf16[3072,512]{1,0:T(8,128)(2,1)}) %all-gather.4.cloned.1.call-update) | async-done | bytes 3145744 | tf_op jit(solution)/shard_map/all_gather | solution.py:49
  134.4 2.8 dynamic-slice_select_fusion.2
  137.2 58.1 %all-gather.6.cloned.1.call-done = bf16[3072,512]{1,0:T(8,128)(2,1)} async-done(((bf16[384,512]{1,0:T(8,128)(2,1)}), bf16[3072,512]{1,0:T(8,128)(2,1)}) %all-gather.6.cloned.1.call-update) | async-done | bytes 3145744 | tf_op jit(solution)/shard_map/all_gather | solution.py:49
  195.3 2.8 dynamic-slice_select_fusion.1
  198.2 92.8 %all-reduce.11.cloned.1.call-done = (bf16[1536,512]{1,0:T(8,128)(2,1)}, bf16[1536,512]{1,0:T(8,128)(2,1)}, bf16[1536,512]{1,0:T(8,128)(2,1)}) async-done(((bf16[1536,512]{1,0:T(8,128)(2,1)}, bf16[1536,512]{1,0:T(8,128)(2,1)}, bf16[1536,512]{1,0:T(8,128)(2,1)}), (bf16[1536,512]{1,0:T(8,128)(2,1)}, bf16[1536,512]{1,0:T(8,128)(2,1)}, bf16[1536,512]{1,0:T(8,128)(2,1)})) %all-reduce.11.cloned.1.call-update) | async-done | bytes 4718608 | tf_op jit(solution)/shard_map/psum | solution.py:17
  291.0 22.2 %convolution_bitcast_fusion = f32[3072,512]{0,1:T(8,128)} fusion(bf16[1536,512]{1,0:T(8,128)(2,1)} %get-tuple-element.18, f32[3072,1536]{1,0:T(8,128)} %param.5), kind=kOutput, calls=%fused_computation.1 | convolution fusion | flops 28991029248 | bytes 26738688 | tf_op jit(solution)/shard_map/dot_general | solution.py:21
  313.4 1.3 copy-done.26
  314.7 21.8 %convolution_bitcast_fusion.2 = f32[3072,512]{0,1:T(8,128)} fusion(bf16[1536,512]{1,0:T(8,128)(2,1)S(1)} %copy-done.26, f32[3072,1536]{1,0:T(8,128)} %param.5), kind=kOutput, calls=%fused_computation.3 | convolution fusion | flops 28991029248 | bytes 26738688 | tf_op jit(solution)/shard_map/dot_general | solution.py:21
  336.5 11.7 reduce-scatter.9.cloned.1.call-start
  348.3 21.9 %convolution_bitcast_fusion.1 = f32[3072,512]{0,1:T(8,128)} fusion(bf16[1536,512]{1,0:T(8,128)(2,1)S(1)} %copy-done.25, f32[3072,1536]{1,0:T(8,128)} %param.5), kind=kOutput, calls=%fused_computation.2 | convolution fusion | flops 28991029248 | bytes 26738688 | tf_op jit(solution)/shard_map/dot_general | solution.py:21
  370.2 61.4 %reduce-scatter.11.cloned.1.call-done = f32[384,512]{0,1:T(8,128)} async-done(((f32[3072,512]{0,1:T(8,128)}), f32[384,512]{0,1:T(8,128)}) %reduce-scatter.11.cloned.1.call-update) | async-done | bytes 786448 | tf_op jit(solution)/shard_map/reduce_scatter | solution.py:53
  431.6 120.7 %reduce-scatter.7.cloned.1.call-done = f32[384,512]{0,1:T(8,128)} async-done(((f32[3072,512]{0,1:T(8,128)}), f32[384,512]{0,1:T(8,128)}) %reduce-scatter.7.cloned.1.call-update) | async-done | bytes 786448 | tf_op jit(solution)/shard_map/reduce_scatter | solution.py:53
  552.4 4.1 convolution_add_fusion.4
  556.5 116.8 %reduce-scatter.9.cloned.1.call-done = f32[384,512]{0,1:T(8,128)} async-done(((f32[3072,512]{0,1:T(8,128)}), f32[384,512]{0,1:T(8,128)}) %reduce-scatter.9.cloned.1.call-update) | async-done | bytes 786448 | tf_op jit(solution)/shard_map/reduce_scatter | solution.py:53
  673.3 3.3 fusion.14
  676.7 1.9 fusion.15
  678.6 1.0 fusion.73
  679.5 3.1 fusion.6
  682.7 4.5 fusion
  687.1 2.1 fusion.64
  689.3 0.4 reduce-scatter.17.cloned.1.call-start
  689.7 20.7 %convolution_bitcast_fusion.3 = f32[1536,512]{0,1:T(8,128)} fusion(bf16[3072,512]{1,0:T(8,128)(2,1)} %all-gather.8.cloned.1.call-done, f32[3072,1536]{1,0:T(8,128)} %param.5), kind=kOutput, calls=%fused_computation.4 | convolution fusion | flops 28991029248 | bytes 25165824 | tf_op jit(solution)/shard_map/dot_general | solution.py:25
  710.5 20.9 %convolution_bitcast_fusion.5 = f32[1536,512]{0,1:T(8,128)} fusion(bf16[3072,512]{1,0:T(8,128)(2,1)} %all-gather.4.cloned.1.call-done, f32[3072,1536]{1,0:T(8,128)} %param.5), kind=kOutput, calls=%fused_computation.6 | convolution fusion | flops 28991029248 | bytes 25165824 | tf_op jit(solution)/shard_map/dot_general | solution.py:25
  731.3 0.2 reduce-scatter.15.cloned.1.call-start
  731.6 21.0 %convolution_bitcast_fusion.4 = f32[1536,512]{0,1:T(8,128)} fusion(bf16[3072,512]{1,0:T(8,128)(2,1)} %all-gather.6.cloned.1.call-done, f32[3072,1536]{1,0:T(8,128)} %param.5), kind=kOutput, calls=%fused_computation.5 | convolution fusion | flops 28991029248 | bytes 25165824 | tf_op jit(solution)/shard_map/dot_general | solution.py:25
  752.6 146.4 %all-reduce.7.cloned.1.call-done = (f32[512,1536]{1,0:T(8,128)}, f32[512,512]{1,0:T(8,128)}, f32[512,1024]{0,1:T(8,128)}) async-done(((f32[512,1536]{1,0:T(8,128)}, f32[512,512]{1,0:T(8,128)}, f32[512,1024]{0,1:T(8,128)}), (f32[512,1536]{1,0:T(8,128)}, f32[512,512]{1,0:T(8,128)}, f32[512,1024]{0,1:T(8,128)})) %all-reduce.7.cloned.1.call-update) | async-done | bytes 6291472 | tf_op jit(solution)/shard_map/psum | solution.py:10
  899.1 2.3 slice.74
  901.4 2.5 copy.65
  903.9 35.1 %reduce-scatter.17.cloned.1.call-done = f32[384,512]{0,1:T(8,128)} async-done(((f32[1536,512]{0,1:T(8,128)}), f32[384,512]{0,1:T(8,128)}) %reduce-scatter.17.cloned.1.call-update) | async-done | bytes 786448 | tf_op jit(solution)/shard_map/reduce_scatter | solution.py:82
  939.0 40.1 %reduce-scatter.13.cloned.1.call-done = f32[384,512]{0,1:T(8,128)} async-done(((f32[1536,512]{0,1:T(8,128)}), f32[384,512]{0,1:T(8,128)}) %reduce-scatter.13.cloned.1.call-update) | async-done | bytes 786448 | tf_op jit(solution)/shard_map/reduce_scatter | solution.py:82
  979.1 4.1 convolution_add_fusion.1
  983.2 36.2 %reduce-scatter.15.cloned.1.call-done = f32[384,512]{0,1:T(8,128)} async-done(((f32[1536,512]{0,1:T(8,128)}), f32[384,512]{0,1:T(8,128)}) %reduce-scatter.15.cloned.1.call-update) | async-done | bytes 786448 | tf_op jit(solution)/shard_map/reduce_scatter | solution.py:82
  1019.4 3.4 fusion.16
  1022.8 1.9 fusion.18
  1024.8 1.6 pad_maximum_fusion.2
  1026.3 3.7 copy.51
  1030.1 3.2 pad_maximum_fusion.1
  1033.2 3.2 copy.50
  1036.5 105.0 %all-reduce.9.cloned.1.call-done = (f32[512,1536]{1,0:T(8,128)}, f32[512,512]{1,0:T(8,128)}, f32[512,1024]{0,1:T(8,128)}) async-done(((f32[512,1536]{1,0:T(8,128)}, f32[512,512]{1,0:T(8,128)}, f32[512,1024]{0,1:T(8,128)}), (f32[512,1536]{1,0:T(8,128)}, f32[512,512]{1,0:T(8,128)}, f32[512,1024]{0,1:T(8,128)})) %all-reduce.9.cloned.1.call-update) | async-done | bytes 6291472 | tf_op jit(solution)/shard_map/psum | solution.py:11
  1141.4 3.6 fusion.34
  1145.0 3.2 bitcast_subtract_fusion.7
  1148.2 1.9 fusion.32
  1150.2 1.9 fusion.27
  1152.1 2.0 fusion.13
  1154.1 1.0 copy-done.8
  1155.0 1.9 fusion.25
  1157.0 3.3 fusion.12
  1160.3 2.3 fusion.20
  1162.6 2.3 fusion.70
  1164.9 2.6 copy.39
  1167.5 5.3 fusion.11
  1172.8 2.0 maximum_bitcast_fusion.1
  1174.7 2.4 copy.49
  1177.2 2.3 maximum_bitcast_fusion.2
  1179.5 0.1 copy-done.17
  1179.6 0.3 copy-done.18
  1179.9 0.3 maximum_bitcast_fusion
  1180.2 5.1 pad_maximum_fusion
  (72 shorter events, 0.8 us)
Async XLA Ops:
  7.2 66.3 %all-gather.8.cloned.1.call-start = ((), (), s32[]{:S(2)}) async-start(), calls=%async_computation.10 | async-start | bytes 3538944 | tf_op jit(solution)/shard_map/all_gather | solution.py:49
  10.6 123.8 %all-gather.4.cloned.1.call-start = ((), (), s32[]{:S(2)}) async-start(), calls=%async_computation.6 | async-start | bytes 3538944 | tf_op jit(solution)/shard_map/all_gather | solution.py:49
  11.4 183.9 %all-gather.6.cloned.1.call-start = ((), (), s32[]{:S(2)}) async-start(), calls=%async_computation.8 | async-start | bytes 3538944 | tf_op jit(solution)/shard_map/all_gather | solution.py:49
  12.1 278.9 %all-reduce.11.cloned.1.call-start = ((), (), s32[]{:S(2)}) async-start(), calls=%async_computation.17 | async-start | bytes 9437184 | tf_op jit(solution)/shard_map/psum | solution.py:17
  198.2 233.5 %reduce-scatter.11.cloned.1.call-start = ((), (), s32[]{:S(2)}) async-start(), calls=%async_computation.11 | async-start | bytes 7077888 | tf_op jit(solution)/shard_map/reduce_scatter | solution.py:53
  313.3 1.4 copy-start.26
  313.3 239.1 %reduce-scatter.7.cloned.1.call-start = ((), (), s32[]{:S(2)}) async-start(), calls=%async_computation.7 | async-start | bytes 7077888 | tf_op jit(solution)/shard_map/reduce_scatter | solution.py:53
  336.5 11.7 copy-start.25
  336.5 336.7 %reduce-scatter.9.cloned.1.call-start = ((), (), s32[]{:S(2)}) async-start(), calls=%async_computation.9 | async-start | bytes 7077888 | tf_op jit(solution)/shard_map/reduce_scatter | solution.py:53
  370.2 182.2 %copy-start = (f32[3,512,512]{2,1,0:T(8,128)S(1)}, f32[3,512,512]{2,1,0:T(8,128)}, u32[]{:S(2)}) copy-start(f32[3,512,512]{2,1,0:T(8,128)} %param.7) | copy-start | bytes 9437188
  370.2 528.9 %all-reduce.7.cloned.1.call-start = ((), (), s32[]{:S(2)}) async-start(), calls=%async_computation.15 | async-start | bytes 12582912 | tf_op jit(solution)/shard_map/psum | solution.py:10
  673.3 3.4 copy-start.23
  673.3 5.3 copy-start.7
  676.6 6.0 copy-start.3
  676.6 2.9 copy-start.22
  678.5 4.1 copy-start.12
  678.5 4.1 copy-start.14
  682.7 4.5 copy-start.21
  689.3 249.7 %reduce-scatter.17.cloned.1.call-start = ((), (), s32[]{:S(2)}) async-start(), calls=%async_computation.14 | async-start | bytes 3932160 | tf_op jit(solution)/shard_map/reduce_scatter | solution.py:82
  710.4 268.7 %reduce-scatter.13.cloned.1.call-start = ((), (), s32[]{:S(2)}) async-start(), calls=%async_computation.12 | async-start | bytes 3932160 | tf_op jit(solution)/shard_map/reduce_scatter | solution.py:82
  731.3 288.1 %reduce-scatter.15.cloned.1.call-start = ((), (), s32[]{:S(2)}) async-start(), calls=%async_computation.13 | async-start | bytes 3932160 | tf_op jit(solution)/shard_map/reduce_scatter | solution.py:82
  752.6 388.8 %all-reduce.9.cloned.1.call-start = ((), (), s32[]{:S(2)}) async-start(), calls=%async_computation.16 | async-start | bytes 12582912 | tf_op jit(solution)/shard_map/psum | solution.py:11
  1019.4 3.4 copy-start.24
  1019.4 5.3 copy-start.13
  1141.4 3.6 copy-start.10
  1141.4 3.6 copy-start.11
  1148.2 3.8 copy-start.1
  1148.2 3.8 copy-start.15
  1148.2 3.8 copy-start.16
  1150.1 12.4 %copy-start.4 = (f32[512,512]{0,1:T(8,128)}, f32[512,512]{0,1:T(8,128)S(1)}, u32[]{:S(2)}) copy-start(f32[512,512]{0,1:T(8,128)S(1)} %fusion.32) | copy-start | bytes 3145732
  1152.1 4.9 copy-start.6
  1154.1 1.0 copy-start.8
  1156.9 5.6 copy-start.5
  1167.5 5.3 copy-start.9
  1167.5 5.3 copy-start.19
  1167.5 5.3 copy-start.20
  1177.1 2.4 copy-start.2
  1177.1 2.5 copy-start.17
  1177.2 2.8 copy-start.18
Sparse Core Ops, SparseCore 0:
  10.7 62.7 all-gather.7
  75.7 58.6 all-gather.3
  136.6 58.6 all-gather.5
  198.3 92.7 all-reduce.10
  313.4 118.1 reduce-scatter.10
  435.1 117.2 reduce-scatter.6
  556.0 117.2 reduce-scatter.8
  689.4 209.6 all-reduce.6
  902.2 36.7 reduce-scatter.16
  941.4 37.7 reduce-scatter.12
  981.7 37.7 reduce-scatter.14
  1021.8 119.6 all-reduce.8
